TPU v7x, 256 devices: a whole 4x4x8 slice. The times are simulated.
256 devices in a mesh: row: 16 (over y_hi, z), col: 16 (over y_lo, x, core).
Axes of the slice: x: 4, y: 4 (y_hi: 2, y_lo: 2; y = y_hi * 2 + y_lo), z: 8, core: 2. Of those that a mesh axis runs over, the one named last changes fastest.
Arguments:
- brick_velocity_stress: float32 [1024, 9, 16, 256], P(('row', 'col')), may hold values from -6 to 6
- brick_relaxation_memory: float32 [1024, 18, 16, 256], P(('row', 'col')), may hold values from -2 to 2
- brick_cell_material: int32 [1024, 16, 256], P(('row', 'col')), may hold values from 0 to 7
- brick_live: int32 [1024], P(('row', 'col')), may hold values from 0 to 1, as said below
- water_state: float32 [4, 512, 512, 128], P(None, 'row', 'col'), may hold values from -6 to 6
- water_material: int32 [512, 512, 128], P('row', 'col'), may hold values from 0 to 7
- material_table: float32 [8, 8], replicated, may hold values from 0.01 to 0.95, as said below
Outputs:
- motion_out: float32 [1024, 9, 16, 256], P(('row', 'col'))
- memory_out: float32 [1024, 18, 16, 256], P(('row', 'col'))
- water_out: float32 [4, 512, 512, 128], P(None, 'row', 'col')
Inputs may be any that keep to these rules, and one draw needn't show every extreme that they name: `brick_live`: tiles j and j + 8 of one row of tiles hold 4 live bricks together; in every row some tile holds 4 or none. `material_table`: column 0 is the buoyancy, 1 the first Lame constant (the bulk modulus of water cells), 2 the shear modulus, 3 to 5 the retentions of the three mechanisms, 6 and 7 the anelastic Lame constant and shear modulus.
All inputs are finite; a program needn't handle non-finite values.
Results may differ from a plain program's by a relative error of at most 0.00011.
Values sent between devices are 32-bit elements; how exact they have to be, the bound alone decides.
A program may use at most 128 MiB of HBM per device.

v0:
```python
import jax
import jax.numpy as jnp
from jax import lax
from jax.experimental import pallas as pl
from jax.experimental.pallas import tpu as pltpu
from jax.sharding import PartitionSpec as P

STEPS = 3
SIDE = 32
EDGE = 16
PLANES = 36
ROWS = 40
LANES = 640
INNER = 512
MESH = pl.DeviceIdType.MESH
F32 = jnp.float32


def lane_pos(shape):
    return lax.broadcasted_iota(jnp.int32, shape, len(shape) - 1)


def row_pos(shape):
    return lax.broadcasted_iota(jnp.int32, shape, len(shape) - 2)


def shift(value, amount, axis):
    amount = amount % value.shape[axis]
    return value if amount == 0 else pltpu.roll(value, amount, axis)


def pick(indices, table, column):
    bits = [(indices & (1 << bit)) != 0 for bit in range(3)]
    values = [table[level, column] for level in range(8)]
    values = [jnp.where(bits[0], values[2 * i + 1], values[2 * i]) for i in range(4)]
    values = [jnp.where(bits[1], values[2 * i + 1], values[2 * i]) for i in range(2)]
    return jnp.where(bits[2], values[1], values[0])


def strip(i):
    return pl.ds(pl.multiple_of(8 * i, 8), 8)


def kernel(
    mvs_in, mem_in, mat_in, live_in, water_in, wmat_in, table,
    motion_out, memory_out, water_out,
    B, G, CF, M, MAT, W, WM,
    tbx, tby, tbc, twx, twy, sbx, sby, swx, swy,
    rbx, rby, rbc, rwx, rwy, ebx, eby, ewx, ewy,
    load_sem, send_sem, recv_sem, xsend_sem, xrecv_sem,
):
    row, col = lax.axis_index("row"), lax.axis_index("col")
    nrow, ncol = lax.axis_size("row"), lax.axis_size("col")
    row_to = (row < nrow - 1, row > 0)
    row_from = (row > 0, row < nrow - 1)
    col_to = (col < ncol - 1, col > 0)
    col_from = (col > 0, col < ncol - 1)
    step_of = (1, -1)
    flat = W.reshape(6 * PLANES * ROWS, 128)

    def line(field, y):
        return pl.ds(field * PLANES * ROWS + y, SIDE, stride=ROWS)

    loads = [
        pltpu.make_async_copy(
            water_in, W.at[pl.ds(0, 4), pl.ds(0, SIDE), pl.ds(0, SIDE)], load_sem.at[0]
        ),
        pltpu.make_async_copy(wmat_in, WM, load_sem.at[1]),
    ]
    for s in range(4):
        rows, lanes = pl.ds(EDGE * (s // 2), EDGE), pl.ds(256 * (s % 2), 256)
        loads.append(
            pltpu.make_async_copy(mat_in.at[s], MAT.at[rows, lanes], load_sem.at[2 + s])
        )
        loads.append(
            pltpu.make_async_copy(
                mvs_in.at[s], B.at[pl.ds(0, 9), rows, lanes], load_sem.at[6 + s]
            )
        )
        loads.append(
            pltpu.make_async_copy(mem_in.at[s], M.at[:, rows, lanes], load_sem.at[10 + s])
        )
    for load in loads:
        load.start()

    barrier = pltpu.get_barrier_semaphore()
    partners = []
    for dr in (-1, 0, 1):
        for dc in (-1, 0, 1):
            if dr or dc:
                there = jnp.logical_and(
                    jnp.logical_and(row + dr >= 0, row + dr < nrow),
                    jnp.logical_and(col + dc >= 0, col + dc < ncol),
                )
                partners.append(there)

                @pl.when(there)
                def _():
                    pl.semaphore_signal(
                        barrier, inc=1, device_id=(row + dr, col + dc), device_id_type=MESH
                    )

    for t in range(2):

        @pl.when(jnp.logical_not(row_from[t]))
        def _():
            rbx[:, t] = jnp.zeros((STEPS, EDGE, INNER), F32)
            rwx[:, t] = jnp.zeros((STEPS, 2, SIDE, 128), F32)
            ebx[t] = jnp.zeros((8, INNER), F32)
            ewx[t] = jnp.zeros((2, SIDE, 128), F32)

        @pl.when(jnp.logical_not(col_from[t]))
        def _():
            rby[:, t] = jnp.zeros((STEPS, SIDE, 256), F32)
            rwy[:, t] = jnp.zeros((STEPS, 2, SIDE, 128), F32)
            eby[t] = jnp.zeros((SIDE, 128), F32)
            ewy[t] = jnp.zeros((2, SIDE, 128), F32)

        for u in range(2):

            @pl.when(jnp.logical_not(jnp.logical_and(row_from[t], col_from[u])))
            def _():
                rbc[:, 2 * t + u] = jnp.zeros((STEPS, 8, 128), F32)

    def remote(src, dst, send, recv, dr, dc):
        return pltpu.make_async_remote_copy(
            src_ref=src, dst_ref=dst, send_sem=send, recv_sem=recv,
            device_id=(row + dr, col + dc), device_id_type=MESH,
        )

    def brick_copies(n):
        out = []
        for t in range(2):
            d = step_of[t]
            out.append((
                remote(tbx.at[n, t], rbx.at[n, t], send_sem.at[n, t], recv_sem.at[n, t], d, 0),
                row_to[t], row_from[t],
            ))
            out.append((
                remote(tby.at[n, t], rby.at[n, t], send_sem.at[n, 2 + t],
                       recv_sem.at[n, 2 + t], 0, d),
                col_to[t], col_from[t],
            ))
            for u in range(2):
                q = 2 * t + u
                out.append((
                    remote(tbc.at[n, q], rbc.at[n, q], send_sem.at[n, 4 + q],
                           recv_sem.at[n, 4 + q], d, step_of[u]),
                    jnp.logical_and(row_to[t], col_to[u]),
                    jnp.logical_and(row_from[t], col_from[u]),
                ))
        return out

    def water_copies(n):
        out = []
        for t in range(2):
            d = step_of[t]
            out.append((
                remote(twx.at[n, t], rwx.at[n, t], send_sem.at[n, 8 + t],
                       recv_sem.at[n, 8 + t], d, 0),
                row_to[t], row_from[t],
            ))
            out.append((
                remote(twy.at[n, t], rwy.at[n, t], send_sem.at[n, 10 + t],
                       recv_sem.at[n, 10 + t], 0, d),
                col_to[t], col_from[t],
            ))
        return out

    def first_water_copies():
        out = []
        for t in range(2):
            d = step_of[t]
            out.append((
                remote(swx.at[t], ewx.at[t], xsend_sem.at[t], xrecv_sem.at[t], d, 0),
                row_to[t], row_from[t],
            ))
            out.append((
                remote(swy.at[t], ewy.at[t], xsend_sem.at[2 + t], xrecv_sem.at[2 + t], 0, d),
                col_to[t], col_from[t],
            ))
        return out

    def first_brick_copies():
        out = []
        for t in range(2):
            d = step_of[t]
            out.append((
                remote(sbx.at[t], ebx.at[t], xsend_sem.at[4 + t], xrecv_sem.at[4 + t], d, 0),
                row_to[t], row_from[t],
            ))
            out.append((
                remote(sby.at[t], eby.at[t], xsend_sem.at[6 + t], xrecv_sem.at[6 + t], 0, d),
                col_to[t], col_from[t],
            ))
        return out

    def start(copies):
        for copy, to, _ in copies:

            @pl.when(to)
            def _():
                copy.start()

    def arrive(copies):
        for copy, _, came in copies:

            @pl.when(came)
            def _():
                copy.wait_recv()

    def sent(copies):
        for copy, to, _ in copies:

            @pl.when(to)
            def _():
                copy.wait_send()

    pair = row_pos((8, INNER))
    tile_lane = lane_pos((SIDE, 128))

    def pack_brick(n):
        for half in range(2):
            down, up = jnp.zeros((8, INNER), F32), jnp.zeros((8, INNER), F32)
            ahead, back = jnp.zeros((SIDE, 128), F32), jnp.zeros((SIDE, 128), F32)
            for j in range(4):
                k = 4 * half + j
                if k == 7:
                    continue
                here = pair // 2 == j
                up = jnp.where(here, shift(B[3 + k, 24:32, 0:INNER], 2 * j - 6, 0), up)
                down = jnp.where(here, shift(B[3 + k, 0:8, 0:INNER], 2 * j, 0), down)
                here = tile_lane // 32 == j
                ahead = jnp.where(
                    here, shift(B[3 + k, 0:SIDE, 384:512], 32 * j - 96, 1), ahead
                )
                back = jnp.where(here, shift(B[3 + k, 0:SIDE, 0:128], 32 * j, 1), back)
            tbx[n, 0, 8 * half:8 * half + 8, :] = up
            tbx[n, 1, 8 * half:8 * half + 8, :] = down
            tby[n, 0, :, 128 * half:128 * half + 128] = ahead
            tby[n, 1, :, 128 * half:128 * half + 128] = back
        lane = lane_pos((8, 128))
        for t in range(2):
            rows = slice(24, 32) if t == 0 else slice(0, 8)
            for u in range(2):
                corner = jnp.zeros((8, 128), F32)
                for k in range(6):
                    tile = B[3 + k, rows, 384:512] if u == 0 else B[3 + k, rows, 0:128]
                    tile = shift(tile, 16 * k - (112 if u == 0 else 0), 1)
                    corner = jnp.where(lane // 16 == k, tile, corner)
                tbc[n, 2 * t + u] = corner

    def unpack_brick(n):
        for k in range(7):
            tile, j = k // 4, k % 4
            rows = slice(8 * tile, 8 * tile + 8)
            before = shift(rbx[n, 0, rows, :], 6 - 2 * j, 0)
            after = shift(rbx[n, 1, rows, :], -2 * j, 0)
            B[3 + k, 32:40, 0:INNER] = jnp.where(pair < 4, after, before)
            lanes = slice(128 * tile, 128 * tile + 128)
            before = shift(rby[n, 0, :, lanes], 96 - 32 * j, 1)
            after = shift(rby[n, 1, :, lanes], -32 * j, 1)
            B[3 + k, 0:SIDE, INNER:LANES] = jnp.where(tile_lane < 64, after, before)
        lane, sub = lane_pos((8, 128)), row_pos((8, 128))
        for k in range(6):
            top = jnp.where(
                lane < 64, shift(rbc[n, 3], -16 * k, 1), shift(rbc[n, 2], 112 - 16 * k, 1)
            )
            bottom = jnp.where(
                lane < 64, shift(rbc[n, 1], -16 * k, 1), shift(rbc[n, 0], 112 - 16 * k, 1)
            )
            B[3 + k, 32:40, INNER:LANES] = jnp.where(sub < 4, top, bottom)

    x_extra = ((B, 0), (B, 1), (B, 2), (G, 3), (G, 0), (G, 4))
    y_extra = ((B, 0), (B, 1), (B, 2), (G, 3), (G, 1), (G, 4))

    def pack_first_brick():
        down, up = jnp.zeros((8, INNER), F32), jnp.zeros((8, INNER), F32)
        ahead, back = jnp.zeros((SIDE, 128), F32), jnp.zeros((SIDE, 128), F32)
        for j in range(6):
            ref, f = x_extra[j]
            up = jnp.where(pair == j, shift(ref[f, 24:32, 0:INNER], j - 7, 0), up)
            down = jnp.where(pair == j, shift(ref[f, 0:8, 0:INNER], j, 0), down)
            ref, f = y_extra[j]
            here = tile_lane // 16 == j
            ahead = jnp.where(here, shift(ref[f, 0:SIDE, 384:512], 16 * j - 112, 1), ahead)
            back = jnp.where(here, shift(ref[f, 0:SIDE, 0:128], 16 * j, 1), back)
        sbx[0], sbx[1], sby[0], sby[1] = up, down, ahead, back

    def unpack_first_brick():
        for j in range(6):
            ref, f = x_extra[j]
            ref[f, 32:40, 0:INNER] = jnp.where(
                pair < 4, shift(ebx[1], -j, 0), shift(ebx[0], 7 - j, 0)
            )
            ref, f = y_extra[j]
            ref[f, 0:SIDE, INNER:LANES] = jnp.where(
                tile_lane < 64, shift(eby[1], -16 * j, 1), shift(eby[0], 112 - 16 * j, 1)
            )

    def pack_water(n):
        for k in range(2):
            twx[n, 0, k] = W[0, 30 + k, 0:SIDE, :]
            twx[n, 1, k] = W[0, k, 0:SIDE, :]
            twy[n, 0, k] = flat[line(0, 30 + k), :]
            twy[n, 1, k] = flat[line(0, k), :]

    def unpack_water(n):
        for k in range(2):
            W[0, 34 + k, 0:SIDE, :] = rwx[n, 0, k]
            W[0, 32 + k, 0:SIDE, :] = rwx[n, 1, k]
            flat[line(0, 38 + k), :] = rwy[n, 0, k]
            flat[line(0, 32 + k), :] = rwy[n, 1, k]

    def pack_first_water():
        for k, (fx, fy) in enumerate(((1, 2), (4, 4))):
            swx[0, k] = W[fx, 31, 0:SIDE, :]
            swx[1, k] = W[fx, 0, 0:SIDE, :]
            swy[0, k] = flat[line(fy, 31), :]
            swy[1, k] = flat[line(fy, 0), :]

    def unpack_first_water():
        for k, (fx, fy) in enumerate(((1, 2), (4, 4))):
            W[fx, 35, 0:SIDE, :] = ewx[0, k]
            W[fx, 32, 0:SIDE, :] = ewx[1, k]
            flat[line(fy, 39), :] = ewy[0, k]
            flat[line(fy, 32), :] = ewy[1, k]

    slab = ((B, 9), (G, 0), (G, 1), (G, 2), (G, 4), (CF, 7))

    def to_slab(field):
        ref, f = slab[field]
        for t in range(4):
            value = jnp.zeros((SIDE, 128), F32)
            for j in range(8):
                moved = shift(flat[line(field, 8 * t + j), :], 16 * j, 1)
                value = jnp.where(tile_lane // 16 == j, moved, value)
            ref[f, 0:SIDE, 128 * t:128 * t + 128] = value

    def from_slab(field):
        ref, f = slab[field]
        for t in range(4):
            value = ref[f, 0:SIDE, 128 * t:128 * t + 128]
            for j in range(8):
                where = line(field, 8 * t + j)
                flat[where, :] = jnp.where(
                    tile_lane < 8, shift(value, -16 * j, 1), flat[where, :]
                )

    plane_lane = lane_pos((SIDE, 128))

    def rise(value):
        forward = jnp.where(plane_lane == 127, 0.0, shift(value, -1, 1))
        return forward - shift(value, 1, 1)

    def across(value, axis, amount):
        return shift(value, -amount, axis) - shift(value, amount, axis)

    def water_step():
        def velocity(x, carry):
            below = lax.rem(x + PLANES - 1, PLANES)
            p, b = W[0, x], W[4, x]
            inner_b = b[0:SIDE]
            W[1, x, 0:SIDE] -= inner_b * (W[0, x + 1, 0:SIDE] - W[0, below, 0:SIDE])
            W[2, x] -= b * across(p, 0, 1)
            W[3, x, 0:SIDE] -= inner_b * rise(p[0:SIDE])
            return carry

        lax.fori_loop(0, SIDE, velocity, 0)
        for x, above, below in ((32, 33, 31), (35, 0, 34)):
            W[1, x, 0:SIDE] -= W[4, x, 0:SIDE] * (W[0, above, 0:SIDE] - W[0, below, 0:SIDE])

        def pressure(x, carry):
            below = lax.rem(x + PLANES - 1, PLANES)
            change = W[1, x + 1, 0:SIDE] - W[1, below, 0:SIDE]
            change = change + across(W[2, x], 0, 1)[0:SIDE] + rise(W[3, x, 0:SIDE])
            W[0, x, 0:SIDE] -= W[5, x, 0:SIDE] * change
            return carry

        lax.fori_loop(0, SIDE, pressure, 0)

    def brick_step():
        def along_x(ref, f, i, width):
            sub = row_pos((8, width))
            here = ref[f, strip(i), 0:width]
            after = ref[f, strip(lax.rem(i + 1, 5)), 0:width]
            before = ref[f, strip(lax.rem(i + 4, 5)), 0:width]
            forward = shift(jnp.where(sub == 0, after, here), -1, 0)
            backward = shift(jnp.where(sub == 7, before, here), 1, 0)
            return forward - backward

        def along_z(value, depth, above, under):
            forward = jnp.where(depth == 15, above, shift(value, -1, 1))
            backward = jnp.where(depth == 0, under, shift(value, 1, 1))
            return forward - backward

        def velocity(i, carry):
            depth = lane_pos((8, LANES)) % 16
            here = strip(i)
            s = [B[3 + k, here, :] for k in range(6)]
            p = B[9, here, :]
            forcing = (
                along_x(B, 3, i, LANES) + across(s[3], 1, 16) + along_z(s[4], depth, 0.0, 0.0),
                along_x(B, 6, i, LANES) + across(s[1], 1, 16) + along_z(s[5], depth, 0.0, 0.0),
                along_x(B, 7, i, LANES) + across(s[5], 1, 16)
                + along_z(s[2], depth, -shift(p, 15, 1), 0.0),
            )
            light = G[3, here, :]
            for k in range(3):
                B[k, here, :] += light * forcing[k]
            light = G[4, here, :]
            G[0, here, :] -= light * along_x(B, 9, i, LANES)
            G[1, here, :] -= light * across(p, 1, 16)
            G[2, here, :] -= light * (
                shift(p, -1, 1) - jnp.where(depth == 0, -shift(s[2], -15, 1), shift(p, 1, 1))
            )
            return carry

        lax.fori_loop(0, 5, velocity, 0)

        def stress(i, carry):
            depth = lane_pos((8, INNER)) % 16
            here = strip(i)
            v = [B[k, here, 0:INNER] for k in range(3)]
            dx = [along_x(B, k, i, INNER) for k in range(3)]
            dy = [across(B[k, here, :], 1, 16)[:, 0:INNER] for k in range(3)]
            dz = [
                along_z(v[k], depth, shift(G[k, here, 0:INNER], 15, 1), 0.0) for k in range(3)
            ]
            w = G[2, here, 0:INNER]
            change = along_x(G, 0, i, INNER) + across(G[1, here, :], 1, 16)[:, 0:INNER]
            change = change + shift(w, -1, 1)
            change = change - jnp.where(depth == 0, shift(v[2], -15, 1), shift(w, 1, 1))
            B[9, here, 0:INNER] -= CF[7, here, :] * change
            strain = (
                dx[0], dy[1], dz[2],
                0.5 * (dy[0] + dx[1]), 0.5 * (dz[0] + dx[2]), 0.5 * (dz[1] + dy[2]),
            )
            dilation = dx[0] + dy[1] + dz[2]
            for k in range(6):
                gain = CF[1, here, :] * strain[k]
                relaxed = CF[6, here, :] * strain[k]
                if k < 3:
                    gain = gain + CF[0, here, :] * dilation
                    relaxed = relaxed + CF[5, here, :] * dilation
                for mechanism in range(3):
                    held = M[6 * mechanism + k, here, :]
                    held = relaxed + CF[2 + mechanism, here, :] * (held - relaxed)
                    M[6 * mechanism + k, here, :] = held
                    gain = gain - held
                B[3 + k, here, 0:INNER] += gain
            return carry

        lax.fori_loop(0, 4, stress, 0)

    loads[0].wait()
    for field in range(4):
        to_slab(field)
    pack_water(0)
    count = partners[0].astype(jnp.int32)
    for there in partners[1:]:
        count = count + there.astype(jnp.int32)
    pl.semaphore_wait(barrier, count)
    start(water_copies(0))
    loads[1].wait()

    def water_params(x, carry):
        kinds = WM[x]
        W[4, x, 0:SIDE] = 0.5 * pick(kinds, table, 0)
        W[5, x, 0:SIDE] = 0.5 * pick(kinds, table, 1)
        return carry

    lax.fori_loop(0, SIDE, water_params, 0)
    pack_first_water()
    start(first_water_copies())
    to_slab(4)
    to_slab(5)
    for load in loads[2:]:
        load.wait()
    live = [live_in[s].astype(F32) for s in range(4)]

    def brick_params(i, carry):
        here = strip(i)
        lane = lane_pos((8, INNER))
        first = jnp.where(i < 2, live[0], live[2])
        second = jnp.where(i < 2, live[1], live[3])
        alive = jnp.where(lane < 256, first, second)
        kinds = MAT[here, :]
        G[3, here, 0:INNER] = 0.5 * alive * pick(kinds, table, 0)
        CF[0, here, :] = 0.5 * alive * pick(kinds, table, 1)
        CF[1, here, :] = alive * pick(kinds, table, 2)
        for mechanism in range(3):
            CF[2 + mechanism, here, :] = pick(kinds, table, 3 + mechanism)
        CF[5, here, :] = 0.5 * alive * pick(kinds, table, 6)
        CF[6, here, :] = alive * pick(kinds, table, 7)
        for k in range(9):
            B[k, here, 0:INNER] = B[k, here, 0:INNER] * alive
        for k in range(18):
            M[k, here, :] = M[k, here, :] * alive
        return carry

    lax.fori_loop(0, 4, brick_params, 0)
    pack_brick(0)
    pack_first_brick()
    start(brick_copies(0))
    start(first_brick_copies())
    arrive(first_water_copies())
    unpack_first_water()

    def step(n, carry):
        arrive(water_copies(n))
        unpack_water(n)
        water_step()

        @pl.when(n < STEPS - 1)
        def _():
            pack_water(n + 1)
            start(water_copies(n + 1))

        @pl.when(n == 0)
        def _():
            arrive(first_brick_copies())
            unpack_first_brick()

        arrive(brick_copies(n))
        unpack_brick(n)
        brick_step()

        @pl.when(n < STEPS - 1)
        def _():
            pack_brick(n + 1)
            start(brick_copies(n + 1))

        return carry

    lax.fori_loop(0, STEPS, step, 0)

    stores = []
    for s in range(4):
        rows, lanes = pl.ds(EDGE * (s // 2), EDGE), pl.ds(256 * (s % 2), 256)
        stores.append(
            pltpu.make_async_copy(
                B.at[pl.ds(0, 9), rows, lanes], motion_out.at[s], load_sem.at[2 + s]
            )
        )
        stores.append(
            pltpu.make_async_copy(M.at[:, rows, lanes], memory_out.at[s], load_sem.at[6 + s])
        )
    for store in stores:
        store.start()
    for field in range(4):
        from_slab(field)
    water_store = pltpu.make_async_copy(
        W.at[pl.ds(0, 4), pl.ds(0, SIDE), pl.ds(0, SIDE)], water_out, load_sem.at[0]
    )
    water_store.start()
    sent(first_water_copies())
    sent(first_brick_copies())
    for n in range(STEPS):
        sent(water_copies(n))
        sent(brick_copies(n))
    for store in stores:
        store.wait()
    water_store.wait()


def body(*args):
    any_space = pl.BlockSpec(memory_space=pl.ANY)
    smem = pl.BlockSpec(memory_space=pltpu.SMEM)
    messages = [
        (STEPS, 2, EDGE, INNER), (STEPS, 2, SIDE, 256), (STEPS, 4, 8, 128),
        (STEPS, 2, 2, SIDE, 128), (STEPS, 2, 2, SIDE, 128),
        (2, 8, INNER), (2, SIDE, 128), (2, 2, SIDE, 128), (2, 2, SIDE, 128),
    ]
    messages = [pltpu.VMEM(shape, F32) for shape in messages]
    return pl.pallas_call(
        kernel,
        out_shape=(
            jax.ShapeDtypeStruct((4, 9, EDGE, 256), F32),
            jax.ShapeDtypeStruct((4, 18, EDGE, 256), F32),
            jax.ShapeDtypeStruct((4, SIDE, SIDE, 128), F32),
        ),
        in_specs=[any_space, any_space, any_space, smem, any_space, any_space, smem],
        out_specs=(any_space, any_space, any_space),
        scratch_shapes=[
            pltpu.VMEM((10, ROWS, LANES), F32),
            pltpu.VMEM((5, ROWS, LANES), F32),
            pltpu.VMEM((8, SIDE, INNER), F32),
            pltpu.VMEM((18, SIDE, INNER), F32),
            pltpu.VMEM((SIDE, INNER), jnp.int32),
            pltpu.VMEM((6, PLANES, ROWS, 128), F32),
            pltpu.VMEM((SIDE, SIDE, 128), jnp.int32),
            *messages,
            *messages,
            pltpu.SemaphoreType.DMA((14,)),
            pltpu.SemaphoreType.DMA((STEPS, 12)),
            pltpu.SemaphoreType.DMA((STEPS, 12)),
            pltpu.SemaphoreType.DMA((8,)),
            pltpu.SemaphoreType.DMA((8,)),
        ],
        compiler_params=pltpu.CompilerParams(
            collective_id=0, has_side_effects=True, vmem_limit_bytes=60 << 20
        ),
        name="ultrasound_steps",
    )(*args)


def solution(mesh):
    return jax.shard_map(
        body,
        mesh=mesh,
        in_specs=(
            P(("row", "col"), None, None, None),
            P(("row", "col"), None, None, None),
            P(("row", "col"), None, None),
            P(("row", "col")),
            P(None, "row", "col", None),
            P("row", "col", None),
            P(),
        ),
        out_specs=(
            P(("row", "col"), None, None, None),
            P(("row", "col"), None, None, None),
            P(None, "row", "col", None),
        ),
        check_vma=False,
    )
```

profile of v0, /device:TPU:24, one launch (start us, length us, event | category | flops | bytes accessed | tf_op | source)
XLA Modules:
  0.0 49.2 jit_solution(14701645390494204601)
XLA Ops:
  0.6 42.8 %ultrasound_steps.1 = (f32[4,9,16,256]{3,2,1,0:T(8,128)}, f32[4,18,16,256]{3,2,1,0:T(8,128)}, f32[4,32,32,128]{3,2,1,0:T(8,128)}) custom-call(f32[4,9,16,256]{3,2,1,0:T(8,128)} %mvs_in.1, f32[4,18,16,256]{3,2,1,0:T(8,128)} %mem_in.1, s32[4,16,256]{2,1,0:T(8,128)} %mat_in.1, s32[4]{0:T(128)} %live_in.1, f32[4,32,32,128]{3,2,1,0:T(8,128)} %water_in.1, ...), custom_call_target="tpu_custom_call" | custom-call | tf_op jit(solution)/shard_map/ultrasound_steps/pallas_call | solution.py:576
  43.4 0.0 copy-start
  43.4 2.1 %copy.13 = f32[4,9,16,256]{3,2,1,0:T(8,128)} copy(f32[4,9,16,256]{3,2,1,0:T(8,128)} %get-tuple-element.6) | data formatting | bytes 1179648
  45.5 2.4 %copy.14 = f32[4,18,16,256]{3,2,1,0:T(8,128)} copy(f32[4,18,16,256]{3,2,1,0:T(8,128)} %get-tuple-element.7) | data formatting | bytes 2359296
  47.9 0.0 copy-done
  47.9 1.3 %copy.15 = f32[4,32,32,128]{3,2,1,0:T(8,128)} copy(f32[4,32,32,128]{3,2,1,0:T(8,128)S(1)} %copy-done) | data formatting | bytes 4194304
Async XLA Ops:
  43.4 4.4 %copy-start = (f32[4,32,32,128]{3,2,1,0:T(8,128)S(1)}, f32[4,32,32,128]{3,2,1,0:T(8,128)}, u32[]{:S(2)}) copy-start(f32[4,32,32,128]{3,2,1,0:T(8,128)} %get-tuple-element.8) | copy-start | bytes 6291460
where the time goes:
time: 49.3 us; the launch traced here: 49.2 us
  Pallas kernels  42.8 us (87%)
  local copies, waits for them, and re-layouts  5.75 us (12%)
  between operations  0.65 us (1%)
    pallas_call x1, Pallas kernels, body(): pl.pallas_call(kernel, out_shape=(jax.ShapeDtypeStruct((4, 9, EDGE, 256),...  42.8 us
    unnamed x5, local copies, waits for them, and re-layouts  5.75 us

commit v1 on v0

v1 whole, which is shorter than its diff:
```python
import jax
import jax.numpy as jnp
from jax import lax
from jax.experimental import pallas as pl
from jax.experimental.pallas import tpu as pltpu
from jax.sharding import PartitionSpec as P

STEPS = 3
SIDE = 32
EDGE = 16
PLANES = 36
DEEP = 56
ROWS = 40
PADDED = 40
MAIN_VMEM = 56_000_000
LANES = 640
INNER = 512
MESH = pl.DeviceIdType.MESH
F32 = jnp.float32


def lane_pos(shape):
    return lax.broadcasted_iota(jnp.int32, shape, len(shape) - 1)


def row_pos(shape):
    return lax.broadcasted_iota(jnp.int32, shape, len(shape) - 2)


def shift(value, amount, axis):
    amount = amount % value.shape[axis]
    return value if amount == 0 else pltpu.roll(value, amount, axis)


def across(value, axis, amount):
    return shift(value, -amount, axis) - shift(value, amount, axis)


def pick(indices, table, column):
    bits = [(indices & (1 << bit)) != 0 for bit in range(3)]
    values = [table[level, column] for level in range(8)]
    values = [jnp.where(bits[0], values[2 * i + 1], values[2 * i]) for i in range(4)]
    values = [jnp.where(bits[1], values[2 * i + 1], values[2 * i]) for i in range(2)]
    return jnp.where(bits[2], values[1], values[0])


def rows_of(i):
    return slice(8 * i, 8 * i + 8)


def along_x(ref, f, i, width):
    sub = row_pos((8, width))
    here = ref[f, rows_of(i), 0:width]
    after = ref[f, rows_of((i + 1) % 5), 0:width]
    before = ref[f, rows_of((i + 4) % 5), 0:width]
    forward = shift(jnp.where(sub == 0, after, here), -1, 0)
    backward = shift(jnp.where(sub == 7, before, here), 1, 0)
    return forward - backward


def along_z(value, depth, above):
    forward = jnp.where(depth == 15, above, shift(value, -1, 1))
    backward = jnp.where(depth == 0, 0.0, shift(value, 1, 1))
    return forward - backward


def brick_velocity(i, V, S, G, L, V_to, G_to):
    depth = lane_pos((8, LANES)) % 16
    here = rows_of(i)
    s = [S[k, here, :] for k in range(6)]
    p = S[6, here, :]
    light = L[0, here, :]
    V_to[0, here, :] = V[0, here, :] + light * (
        along_x(S, 0, i, LANES) + across(s[3], 1, 16) + along_z(s[4], depth, 0.0)
    )
    V_to[1, here, :] = V[1, here, :] + light * (
        along_x(S, 3, i, LANES) + across(s[1], 1, 16) + along_z(s[5], depth, 0.0)
    )
    V_to[2, here, :] = V[2, here, :] + light * (
        along_x(S, 4, i, LANES) + across(s[5], 1, 16)
        + along_z(s[2], depth, -shift(p, 15, 1))
    )
    light = L[1, here, :]
    G_to[0, here, :] = G[0, here, :] - light * along_x(S, 6, i, LANES)
    G_to[1, here, :] = G[1, here, :] - light * across(p, 1, 16)
    G_to[2, here, :] = G[2, here, :] - light * (
        shift(p, -1, 1) - jnp.where(depth == 0, -shift(s[2], -15, 1), shift(p, 1, 1))
    )


def brick_stress(i, V, S, G, CF, M, S_to, M_to):
    depth = lane_pos((8, INNER)) % 16
    here = rows_of(i)
    v = [V[k, here, 0:INNER] for k in range(3)]
    w = G[2, here, 0:INNER]
    change = along_x(G, 0, i, INNER) + across(G[1, here, :], 1, 16)[:, 0:INNER]
    change = change + shift(w, -1, 1)
    change = change - jnp.where(depth == 0, shift(v[2], -15, 1), shift(w, 1, 1))
    S_to[6, here, 0:INNER] = S[6, here, 0:INNER] - CF[7, here, :] * change
    dx = [along_x(V, k, i, INNER) for k in range(3)]
    dy = [across(V[k, here, :], 1, 16)[:, 0:INNER] for k in range(3)]
    dz = [along_z(v[k], depth, shift(G[k, here, 0:INNER], 15, 1)) for k in range(3)]
    strain = (
        dx[0], dy[1], dz[2],
        0.5 * (dy[0] + dx[1]), 0.5 * (dz[0] + dx[2]), 0.5 * (dz[1] + dy[2]),
    )
    dilation = dx[0] + dy[1] + dz[2]
    for k in range(6):
        gain = CF[1, here, :] * strain[k]
        relaxed = CF[6, here, :] * strain[k]
        if k < 3:
            gain = gain + CF[0, here, :] * dilation
            relaxed = relaxed + CF[5, here, :] * dilation
        for mechanism in range(3):
            held = M[6 * mechanism + k, here, :]
            held = relaxed + CF[2 + mechanism, here, :] * (held - relaxed)
            M_to[6 * mechanism + k, here, :] = held
            gain = gain - held
        S_to[k, here, 0:INNER] = S[k, here, 0:INNER] + gain


def main_kernel(
    mvs_in, mem_in, mat_in, live_in, water_in, wmat_in, table,
    V, S, G, L, CF, M, PR, U,
    C, MAT, WS, WM,
    tbx, tby, tbc, twx, twy, sbx, sby, swx, swy,
    rbx, rby, rbc, rwx, rwy, ebx, eby, ewx, ewy,
    load_sem, send_sem, recv_sem, xsend_sem, xrecv_sem,
):
    row, col = lax.axis_index("row"), lax.axis_index("col")
    nrow, ncol = lax.axis_size("row"), lax.axis_size("col")
    row_to = (row < nrow - 1, row > 0)
    row_from = (row > 0, row < nrow - 1)
    col_to = (col < ncol - 1, col > 0)
    col_from = (col > 0, col < ncol - 1)
    step_of = (1, -1)
    inner = pl.ds(8, SIDE)

    def line(field, y):
        return pl.ds(field * PLANES * DEEP + 2 * DEEP + 8 + y, SIDE, stride=DEEP)

    flat_p = PR.reshape(PLANES * DEEP, 128)
    flat_u = U.reshape(3 * PLANES * DEEP, 128)
    flat_c = C.reshape(3 * PLANES * DEEP, 128)
    flat_m = WM.reshape(SIDE * PADDED, 128)

    loads, motion_loads, memory_loads = [], [], []
    for s in range(4):
        rows, lanes = pl.ds(EDGE * (s // 2), EDGE), pl.ds(256 * (s % 2), 256)
        motion_loads += [
            pltpu.make_async_copy(
                mvs_in.at[s, pl.ds(0, 3)], V.at[:, rows, lanes], load_sem.at[s]
            ),
            pltpu.make_async_copy(
                mvs_in.at[s, pl.ds(3, 6)], S.at[pl.ds(0, 6), rows, lanes], load_sem.at[4 + s]
            ),
            pltpu.make_async_copy(mat_in.at[s], MAT.at[rows, lanes], load_sem.at[8 + s]),
        ]
        memory_loads.append(
            pltpu.make_async_copy(mem_in.at[s], M.at[:, rows, lanes], load_sem.at[12 + s])
        )
    pressure_load = pltpu.make_async_copy(
        water_in.at[0], PR.at[pl.ds(2, SIDE), inner], load_sem.at[16]
    )
    velocity_load = pltpu.make_async_copy(
        water_in.at[pl.ds(1, 3)], U.at[:, pl.ds(2, SIDE), inner], load_sem.at[17]
    )
    kind_load = pltpu.make_async_copy(
        wmat_in, WM.at[:, pl.ds(0, SIDE)], load_sem.at[18]
    )
    for load in motion_loads + [pressure_load, velocity_load, kind_load] + memory_loads:
        load.start()

    barrier = pltpu.get_barrier_semaphore()
    partners = []
    for dr in (-1, 0, 1):
        for dc in (-1, 0, 1):
            if dr or dc:
                there = jnp.logical_and(
                    jnp.logical_and(row + dr >= 0, row + dr < nrow),
                    jnp.logical_and(col + dc >= 0, col + dc < ncol),
                )
                partners.append(there)

                @pl.when(there)
                def _():
                    pl.semaphore_signal(
                        barrier, inc=1, device_id=(row + dr, col + dc), device_id_type=MESH
                    )

    for t in range(2):

        @pl.when(jnp.logical_not(row_from[t]))
        def _():
            rbx[:, t] = jnp.zeros((STEPS, EDGE, INNER), F32)
            rwx[:, t] = jnp.zeros((STEPS, 2, SIDE, 128), F32)
            ebx[t] = jnp.zeros((8, INNER), F32)
            ewx[t] = jnp.zeros((2, SIDE, 128), F32)

        @pl.when(jnp.logical_not(col_from[t]))
        def _():
            rby[:, t] = jnp.zeros((STEPS, SIDE, 256), F32)
            rwy[:, t] = jnp.zeros((STEPS, 2, SIDE, 128), F32)
            eby[t] = jnp.zeros((SIDE, 128), F32)
            ewy[t] = jnp.zeros((2, SIDE, 128), F32)

        for u in range(2):

            @pl.when(jnp.logical_not(jnp.logical_and(row_from[t], col_from[u])))
            def _():
                rbc[:, 2 * t + u] = jnp.zeros((STEPS, 8, 128), F32)

    def remote(src, dst, send, recv, dr, dc):
        return pltpu.make_async_remote_copy(
            src_ref=src, dst_ref=dst, send_sem=send, recv_sem=recv,
            device_id=(row + dr, col + dc), device_id_type=MESH,
        )

    def brick_x_copies(n):
        out = []
        for t in range(2):
            d = step_of[t]
            out.append((
                remote(tbx.at[n, t], rbx.at[n, t], send_sem.at[n, t], recv_sem.at[n, t], d, 0),
                row_to[t], row_from[t],
            ))
            for u in range(2):
                q = 2 * t + u
                out.append((
                    remote(tbc.at[n, q], rbc.at[n, q], send_sem.at[n, 4 + q],
                           recv_sem.at[n, 4 + q], d, step_of[u]),
                    jnp.logical_and(row_to[t], col_to[u]),
                    jnp.logical_and(row_from[t], col_from[u]),
                ))
        return out

    def side_copies(x_refs, y_refs, x_sems, y_sems):
        out = []
        for t in range(2):
            d = step_of[t]
            if x_refs:
                out.append((
                    remote(x_refs[0].at[t], x_refs[1].at[t], x_sems[0](t), x_sems[1](t), d, 0),
                    row_to[t], row_from[t],
                ))
            if y_refs:
                out.append((
                    remote(y_refs[0].at[t], y_refs[1].at[t], y_sems[0](t), y_sems[1](t), 0, d),
                    col_to[t], col_from[t],
                ))
        return out

    def step_sems(n, first):
        return (lambda t: send_sem.at[n, first + t]), (lambda t: recv_sem.at[n, first + t])

    def extra_sems(first):
        return (lambda t: xsend_sem.at[first + t]), (lambda t: xrecv_sem.at[first + t])

    def brick_y_copies(n):
        return side_copies(None, (tby.at[n], rby.at[n]), None, step_sems(n, 2))

    def water_copies(n):
        return side_copies(
            (twx.at[n], rwx.at[n]), (twy.at[n], rwy.at[n]), step_sems(n, 8), step_sems(n, 10)
        )

    def first_water_copies():
        return side_copies((swx, ewx), (swy, ewy), extra_sems(0), extra_sems(2))

    def first_brick_copies():
        return side_copies((sbx, ebx), (sby, eby), extra_sems(4), extra_sems(6))

    def start(copies):
        for copy, to, _ in copies:

            @pl.when(to)
            def _():
                copy.start()

    def arrive(copies):
        for copy, _, came in copies:

            @pl.when(came)
            def _():
                copy.wait_recv()

    def sent(copies):
        for copy, to, _ in copies:

            @pl.when(to)
            def _():
                copy.wait_send()

    pair = row_pos((8, INNER))
    tile_lane = lane_pos((SIDE, 128))
    lane, sub = lane_pos((8, 128)), row_pos((8, 128))

    def pack_brick_x(n):
        for half in range(2):
            down, up = jnp.zeros((8, INNER), F32), jnp.zeros((8, INNER), F32)
            for j in range(3 if half else 4):
                k = 4 * half + j
                here = pair // 2 == j
                up = jnp.where(here, shift(S[k, 24:32, 0:INNER], 2 * j - 6, 0), up)
                down = jnp.where(here, shift(S[k, 0:8, 0:INNER], 2 * j, 0), down)
            tbx[n, 0, 8 * half:8 * half + 8, :] = up
            tbx[n, 1, 8 * half:8 * half + 8, :] = down
        for t in range(2):
            rows = slice(24, 32) if t == 0 else slice(0, 8)
            for u in range(2):
                corner = jnp.zeros((8, 128), F32)
                for k in range(6):
                    tile = S[k, rows, 384:512] if u == 0 else S[k, rows, 0:128]
                    tile = shift(tile, 16 * k - (112 if u == 0 else 0), 1)
                    corner = jnp.where(lane // 16 == k, tile, corner)
                tbc[n, 2 * t + u] = corner

    def pack_brick_y(n):
        for half in range(2):
            ahead, back = jnp.zeros((SIDE, 128), F32), jnp.zeros((SIDE, 128), F32)
            for j in range(3 if half else 4):
                k = 4 * half + j
                here = tile_lane // 32 == j
                ahead = jnp.where(here, shift(S[k, 0:SIDE, 384:512], 32 * j - 96, 1), ahead)
                back = jnp.where(here, shift(S[k, 0:SIDE, 0:128], 32 * j, 1), back)
            tby[n, 0, :, 128 * half:128 * half + 128] = ahead
            tby[n, 1, :, 128 * half:128 * half + 128] = back

    def unpack_brick_x(n):
        for k in range(7):
            tile, j = k // 4, k % 4
            rows = rows_of(tile)
            before = shift(rbx[n, 0, rows, :], 6 - 2 * j, 0)
            after = shift(rbx[n, 1, rows, :], -2 * j, 0)
            S[k, 32:40, 0:INNER] = jnp.where(pair < 4, after, before)
        for k in range(6):
            top = jnp.where(
                lane < 64, shift(rbc[n, 3], -16 * k, 1), shift(rbc[n, 2], 112 - 16 * k, 1)
            )
            bottom = jnp.where(
                lane < 64, shift(rbc[n, 1], -16 * k, 1), shift(rbc[n, 0], 112 - 16 * k, 1)
            )
            S[k, 32:40, INNER:LANES] = jnp.where(sub < 4, top, bottom)

    def unpack_brick_y(n):
        for k in range(7):
            tile, j = k // 4, k % 4
            lanes = slice(128 * tile, 128 * tile + 128)
            before = shift(rby[n, 0, :, lanes], 96 - 32 * j, 1)
            after = shift(rby[n, 1, :, lanes], -32 * j, 1)
            S[k, 0:SIDE, INNER:LANES] = jnp.where(tile_lane < 64, after, before)

    x_extra = ((V, 0), (V, 1), (V, 2), (L, 0), (G, 0), (L, 1))
    y_extra = ((V, 0), (V, 1), (V, 2), (L, 0), (G, 1), (L, 1))

    def pack_first_brick():
        down, up = jnp.zeros((8, INNER), F32), jnp.zeros((8, INNER), F32)
        ahead, back = jnp.zeros((SIDE, 128), F32), jnp.zeros((SIDE, 128), F32)
        for j in range(6):
            ref, f = x_extra[j]
            up = jnp.where(pair == j, shift(ref[f, 24:32, 0:INNER], j - 7, 0), up)
            down = jnp.where(pair == j, shift(ref[f, 0:8, 0:INNER], j, 0), down)
            ref, f = y_extra[j]
            here = tile_lane // 16 == j
            ahead = jnp.where(here, shift(ref[f, 0:SIDE, 384:512], 16 * j - 112, 1), ahead)
            back = jnp.where(here, shift(ref[f, 0:SIDE, 0:128], 16 * j, 1), back)
        sbx[0], sbx[1], sby[0], sby[1] = up, down, ahead, back

    def unpack_first_brick():
        for j in range(6):
            ref, f = x_extra[j]
            ref[f, 32:40, 0:INNER] = jnp.where(
                pair < 4, shift(ebx[1], -j, 0), shift(ebx[0], 7 - j, 0)
            )
            ref, f = y_extra[j]
            ref[f, 0:SIDE, INNER:LANES] = jnp.where(
                tile_lane < 64, shift(eby[1], -16 * j, 1), shift(eby[0], 112 - 16 * j, 1)
            )

    def pack_water(n):
        for k in range(2):
            twx[n, 0, k] = PR[32 + k, inner, :]
            twx[n, 1, k] = PR[2 + k, inner, :]
            twy[n, 0, k] = flat_p[line(0, 30 + k), :]
            twy[n, 1, k] = flat_p[line(0, k), :]

    def unpack_water(n):
        for k in range(2):
            PR[k, inner, :] = rwx[n, 0, k]
            PR[34 + k, inner, :] = rwx[n, 1, k]
            flat_p[line(0, k - 2), :] = rwy[n, 0, k]
            flat_p[line(0, 32 + k), :] = rwy[n, 1, k]

    def pack_first_water():
        swx[0, 0], swx[0, 1] = U[0, 33, inner, :], C[0, 33, inner, :]
        swx[1, 0], swx[1, 1] = U[0, 2, inner, :], C[0, 2, inner, :]
        swy[0, 0], swy[0, 1] = flat_u[line(1, 31), :], flat_c[line(0, 31), :]
        swy[1, 0], swy[1, 1] = flat_u[line(1, 0), :], flat_c[line(0, 0), :]

    def unpack_first_water():
        U[0, 1, inner, :], C[0, 1, inner, :] = ewx[0, 0], ewx[0, 1]
        U[0, 34, inner, :], C[0, 34, inner, :] = ewx[1, 0], ewx[1, 1]
        flat_u[line(1, -1), :], flat_c[line(0, -1), :] = ewy[0, 0], ewy[0, 1]
        flat_u[line(1, 32), :], flat_c[line(0, 32), :] = ewy[1, 0], ewy[1, 1]

    def to_slab(ref, f, rows_at):
        for t in range(4):
            value = rows_at(8 * t)
            for j in range(1, 8):
                moved = shift(rows_at(8 * t + j), 16 * j, 1)
                value = jnp.where(tile_lane // 16 == j, moved, value)
            if f is None:
                ref[:, 128 * t:128 * t + 128] = value
            else:
                ref[f, 0:SIDE, 128 * t:128 * t + 128] = value

    plane_lane = lane_pos((SIDE, 128))
    wide, above_rows, below_rows = pl.ds(7, 40), pl.ds(8, 40), pl.ds(6, 40)

    def water_step():
        def velocity(x, carry):
            for plane in range(4):
                x_at = 4 * x + (2 + plane)
                p, light = PR[x_at, inner], C[0, x_at, inner]
                U[0, x_at, inner] -= light * (PR[x_at + 1, inner] - PR[x_at - 1, inner])
                U[1, x_at, wide] -= C[0, x_at, wide] * (
                    PR[x_at, above_rows] - PR[x_at, below_rows]
                )
                U[2, x_at, inner] -= C[2, x_at, inner] * (
                    jnp.where(plane_lane == 0, 0.0, p) - shift(p, 2, 1)
                )
            return carry

        lax.fori_loop(0, SIDE // 4, velocity, 0)
        for x_at in (1, 34):
            U[0, x_at, inner] -= C[0, x_at, inner] * (
                PR[x_at + 1, inner] - PR[x_at - 1, inner]
            )

        def pressure(x, carry):
            for plane in range(4):
                x_at = 4 * x + (2 + plane)
                change = U[0, x_at + 1, inner] - U[0, x_at - 1, inner]
                change = change + (U[1, x_at, pl.ds(9, SIDE)] - U[1, x_at, pl.ds(7, SIDE)])
                w = U[2, x_at, inner]
                change = change + (jnp.where(plane_lane == 127, 0.0, shift(w, -2, 1)) - w)
                PR[x_at, inner] -= C[1, x_at, inner] * change
            return carry

        lax.fori_loop(0, SIDE // 4, pressure, 0)

    for load in motion_loads:
        load.wait()
    live = [live_in[s].astype(F32) for s in range(4)]

    def alive_of(i):
        left = lane_pos((8, INNER)) < 256
        return jnp.where(
            left, jnp.where(i < 2, live[0], live[2]), jnp.where(i < 2, live[1], live[3])
        )

    def strip(i):
        return pl.ds(pl.multiple_of(8 * i, 8), 8)

    def motion_start(i, carry):
        here = strip(i)
        alive = alive_of(i)
        for k in range(3):
            V[k, here, 0:INNER] = V[k, here, 0:INNER] * alive
        for k in range(6):
            S[k, here, 0:INNER] = S[k, here, 0:INNER] * alive
        L[0, here, 0:INNER] = 0.5 * alive * pick(MAT[here, :], table, 0)
        return carry

    lax.fori_loop(0, 4, motion_start, 0)
    pressure_load.wait()
    to_slab(S, 6, lambda y: flat_p[line(0, y), :])
    pack_brick_x(0)
    pack_brick_y(0)
    count = partners[0].astype(jnp.int32)
    for there in partners[1:]:
        count = count + there.astype(jnp.int32)
    pl.semaphore_wait(barrier, count)
    start(brick_x_copies(0))
    start(brick_y_copies(0))
    velocity_load.wait()
    kind_load.wait()
    to_slab(G, 0, lambda y: flat_u[line(0, y), :])
    to_slab(G, 1, lambda y: flat_u[line(1, y), :])
    to_slab(WS, None, lambda y: flat_m[pl.ds(y, SIDE, stride=PADDED), :])

    def slab_params(i, carry):
        here = strip(i)
        L[1, here, 0:INNER] = 0.5 * pick(WS[here, :], table, 0)
        CF[7, here, :] = 0.5 * pick(WS[here, :], table, 1)
        return carry

    lax.fori_loop(0, 4, slab_params, 0)
    pack_first_brick()
    start(first_brick_copies())
    pack_water(0)
    start(water_copies(0))
    to_slab(G, 2, lambda y: flat_u[line(2, y), :])

    def water_params(x, carry):
        for plane in range(2):
            kinds = WM[2 * x + plane, 0:SIDE]
            x_at = 2 * x + (2 + plane)
            light = 0.5 * pick(kinds, table, 0)
            C[0, x_at, inner] = light
            C[1, x_at, inner] = 0.5 * pick(kinds, table, 1)
            C[2, x_at, inner] = shift(light, 1, 1)
            U[2, x_at, inner] = shift(U[2, x_at, inner], 1, 1)
        return carry

    lax.fori_loop(0, SIDE // 2, water_params, 0)
    pack_first_water()
    start(first_water_copies())
    for load in memory_loads:
        load.wait()

    def memory_start(i, carry):
        here = strip(i)
        alive = alive_of(i)
        kinds = MAT[here, :]
        CF[0, here, :] = 0.5 * alive * pick(kinds, table, 1)
        CF[1, here, :] = alive * pick(kinds, table, 2)
        for mechanism in range(3):
            CF[2 + mechanism, here, :] = pick(kinds, table, 3 + mechanism)
        CF[5, here, :] = 0.5 * alive * pick(kinds, table, 6)
        CF[6, here, :] = alive * pick(kinds, table, 7)
        for k in range(18):
            M[k, here, :] = M[k, here, :] * alive
        return carry

    lax.fori_loop(0, 4, memory_start, 0)
    arrive(first_water_copies())
    unpack_first_water()

    def step(n, carry):
        arrive(water_copies(n))
        unpack_water(n)
        water_step()
        pack_water(n + 1)
        start(water_copies(n + 1))

        @pl.when(n == 0)
        def _():
            arrive(first_brick_copies())
            unpack_first_brick()

        arrive(brick_y_copies(n))
        unpack_brick_y(n)
        for i in (1, 2):
            brick_velocity(i, V, S, G, L, V, G)
        arrive(brick_x_copies(n))
        unpack_brick_x(n)
        for i in (0, 3, 4):
            brick_velocity(i, V, S, G, L, V, G)
        for i in (0, 3):
            brick_stress(i, V, S, G, CF, M, S, M)
        pack_brick_x(n + 1)
        start(brick_x_copies(n + 1))
        for i in (1, 2):
            brick_stress(i, V, S, G, CF, M, S, M)
        pack_brick_y(n + 1)
        start(brick_y_copies(n + 1))
        return carry

    lax.fori_loop(0, STEPS - 1, step, 0)
    last = STEPS - 1
    arrive(water_copies(last))
    unpack_water(last)
    water_step()

    def settle(x, carry):
        for plane in range(4):
            x_at = 4 * x + (2 + plane)
            U[2, x_at, inner] = shift(U[2, x_at, inner], -1, 1)
        return carry

    lax.fori_loop(0, SIDE // 4, settle, 0)
    sent(first_water_copies())
    sent(first_brick_copies())
    for n in range(STEPS):
        sent(water_copies(n))
        sent(brick_x_copies(n))
        sent(brick_y_copies(n))
    arrive(brick_y_copies(last))
    unpack_brick_y(last)
    arrive(brick_x_copies(last))
    unpack_brick_x(last)


def last_kernel(
    V, S, G, L, CF, M, PR, U,
    motion_out, memory_out, water_out,
    V_to, G_to, S_to, M_to, W_to, sem,
):
    for i in range(5):
        brick_velocity(i, V, S, G, L, V_to, G_to)
    for i in range(4):
        brick_stress(i, V_to, S, G_to, CF, M, S_to, M_to)
    stores = []
    for s in range(4):
        rows, lanes = pl.ds(EDGE * (s // 2), EDGE), pl.ds(256 * (s % 2), 256)
        stores += [
            pltpu.make_async_copy(
                V_to.at[:, rows, lanes], motion_out.at[s, pl.ds(0, 3)], sem.at[s]
            ),
            pltpu.make_async_copy(
                S_to.at[pl.ds(0, 6), rows, lanes], motion_out.at[s, pl.ds(3, 6)], sem.at[4 + s]
            ),
            pltpu.make_async_copy(M_to.at[:, rows, lanes], memory_out.at[s], sem.at[8 + s]),
        ]
    for store in stores:
        store.start()
    tile_lane = lane_pos((SIDE, 128))
    flat_p = PR.reshape(PLANES * DEEP, 128)
    flat_u = U.reshape(3 * PLANES * DEEP, 128)
    flat_to = W_to.reshape(4 * SIDE * PADDED, 128)
    for field in range(4):
        ref, f = ((S_to, 6), (G_to, 0), (G_to, 1), (G_to, 2))[field]
        main = flat_p if field == 0 else flat_u
        base = 2 * DEEP + 8 + max(field - 1, 0) * PLANES * DEEP
        for t in range(4):
            value = ref[f, 0:SIDE, 128 * t:128 * t + 128]
            for j in range(8):
                y = 8 * t + j
                flat_to[pl.ds(field * SIDE * PADDED + y, SIDE, stride=PADDED), :] = jnp.where(
                    tile_lane < 8,
                    shift(value, -16 * j, 1),
                    main[pl.ds(base + y, SIDE, stride=DEEP), :],
                )
        stores.append(
            pltpu.make_async_copy(
                W_to.at[field, :, pl.ds(0, SIDE)], water_out.at[field], sem.at[12 + field]
            )
        )
        stores[-1].start()
    for store in stores:
        store.wait()


def body(*args):
    any_space = pl.BlockSpec(memory_space=pltpu.HBM)
    smem = pl.BlockSpec(memory_space=pltpu.SMEM)
    vmem = pl.BlockSpec(memory_space=pltpu.VMEM)
    messages = [
        (STEPS, 2, EDGE, INNER), (STEPS, 2, SIDE, 256), (STEPS, 4, 8, 128),
        (STEPS, 2, 2, SIDE, 128), (STEPS, 2, 2, SIDE, 128),
        (2, 8, INNER), (2, SIDE, 128), (2, 2, SIDE, 128), (2, 2, SIDE, 128),
    ]
    messages = [pltpu.VMEM(shape, F32) for shape in messages]
    state = [
        (3, ROWS, LANES), (7, ROWS, LANES), (3, ROWS, LANES), (2, ROWS, LANES),
        (8, SIDE, INNER), (18, SIDE, INNER),
        (PLANES, DEEP, 128), (3, PLANES, DEEP, 128),
    ]
    held = pl.pallas_call(
        main_kernel,
        out_shape=tuple(pltpu.VMEM(shape, F32) for shape in state),
        in_specs=[any_space, any_space, any_space, smem, any_space, any_space, smem],
        out_specs=(vmem,) * len(state),
        scratch_shapes=[
            pltpu.VMEM((3, PLANES, DEEP, 128), F32),
            pltpu.VMEM((SIDE, INNER), jnp.int32),
            pltpu.VMEM((SIDE, INNER), jnp.int32),
            pltpu.VMEM((SIDE, PADDED, 128), jnp.int32),
            *messages,
            *messages,
            pltpu.SemaphoreType.DMA((19,)),
            pltpu.SemaphoreType.DMA((STEPS, 12)),
            pltpu.SemaphoreType.DMA((STEPS, 12)),
            pltpu.SemaphoreType.DMA((8,)),
            pltpu.SemaphoreType.DMA((8,)),
        ],
        compiler_params=pltpu.CompilerParams(
            collective_id=0, has_side_effects=True, vmem_limit_bytes=MAIN_VMEM
        ),
        name="ultrasound_steps",
    )(*args)
    return pl.pallas_call(
        last_kernel,
        out_shape=(
            jax.ShapeDtypeStruct((4, 9, EDGE, 256), F32),
            jax.ShapeDtypeStruct((4, 18, EDGE, 256), F32),
            jax.ShapeDtypeStruct((4, SIDE, SIDE, 128), F32),
        ),
        in_specs=[vmem] * 8,
        out_specs=(any_space,) * 3,
        scratch_shapes=[
            pltpu.VMEM((3, ROWS, LANES), F32),
            pltpu.VMEM((3, ROWS, LANES), F32),
            pltpu.VMEM((7, SIDE, INNER), F32),
            pltpu.VMEM((18, SIDE, INNER), F32),
            pltpu.VMEM((4, SIDE, PADDED, 128), F32),
            pltpu.SemaphoreType.DMA((16,)),
        ],
        compiler_params=pltpu.CompilerParams(vmem_limit_bytes=24 << 20),
        name="ultrasound_last",
    )(*held)


def solution(mesh):
    return jax.shard_map(
        body,
        mesh=mesh,
        in_specs=(
            P(("row", "col"), None, None, None),
            P(("row", "col"), None, None, None),
            P(("row", "col"), None, None),
            P(("row", "col")),
            P(None, "row", "col", None),
            P("row", "col", None),
            P(),
        ),
        out_specs=(
            P(("row", "col"), None, None, None),
            P(("row", "col"), None, None, None),
            P(None, "row", "col", None),
        ),
        check_vma=False,
    )
```

time: 49.3 us -> 34.5 us (0.70)
  Pallas kernels: 42.8 us -> 33.7 us
  local copies, waits for them, and re-layouts: 5.75 us -> 0 us
    pallas_call x1 -> x2, Pallas kernels: 42.8 us -> 33.7 us  [the longest x1 30.7 us: body(): pl.pallas_call(main_kernel, out_shape=tuple((pltpu.VMEM(shape, F32) for s...]
    unnamed x5 -> x0, local copies, waits for them, and re-layouts: 5.75 us -> none
where the time goes in v1:
time: 34.5 us; the launch traced here: 34.4 us
  Pallas kernels  33.7 us (98%)
  between operations  0.64 us (2%)
    pallas_call x1, Pallas kernels, body(): pl.pallas_call(main_kernel, out_shape=tuple((pltpu.VMEM(shape, F32) for s...  30.7 us
    pallas_call x1, Pallas kernels, body(): pl.pallas_call(last_kernel, out_shape=(jax.ShapeDtypeStruct((4, 9, EDGE,...  3.06 us

profile of v1, /device:TPU:24, one launch (start us, length us, event | category | flops | bytes accessed | tf_op | source)
XLA Modules:
  0.0 34.4 jit_solution(5400084841552909738)
XLA Ops:
  0.6 30.7 %ultrasound_steps.1 = (f32[3,40,640]{2,1,0:T(8,128)S(1)}, f32[7,40,640]{2,1,0:T(8,128)S(1)}, f32[3,40,640]{2,1,0:T(8,128)S(1)}, f32[2,40,640]{2,1,0:T(8,128)S(1)...) custom-call(f32[4,9,16,256]{3,2,1,0:T(8,128)} %mvs_in.1, ...), custom_call_target="tpu_custom_call" | custom-call | tf_op jit(solution)/shard_map/ultrasound_steps/pallas_call | solution.py:660
  31.3 3.1 %ultrasound_last.1 = (f32[4,9,16,256]{3,2,1,0:T(8,128)}, f32[4,18,16,256]{3,2,1,0:T(8,128)}, f32[4,32,32,128]{3,2,1,0:T(8,128)}) custom-call(f32[3,40,640]{2,1,0:T(8,128)S(1)} %get-tuple-element.11.V, f32[7,40,640]{2,1,0:T(8,128)S(1)} %get-tuple-element.12.S, f32[3,40,640]{2,1,0:T(8,128)S(1)} %get-tuple-element.13.G, f32[2,40,640]{2,1,0:T(8,128)S(1)} %get-tuple-element.14.L, ...), custom_call_target="tpu_custom_call" | custom-call | tf_op jit(solution)/shard_map/ultrasound_last/pallas_call | solution.py:683

commit v2 on v1

--- a/solution.py
+++ b/solution.py
@@ -17,6 +17,7 @@
 INNER = 512
 MESH = pl.DeviceIdType.MESH
 F32 = jnp.float32
+BF16 = jnp.bfloat16
 
 
 def lane_pos(shape):
@@ -58,71 +59,121 @@
     return forward - backward
 
 
-def along_z(value, depth, above):
-    forward = jnp.where(depth == 15, above, shift(value, -1, 1))
-    backward = jnp.where(depth == 0, 0.0, shift(value, 1, 1))
-    return forward - backward
-
-
-def brick_velocity(i, V, S, G, L, V_to, G_to):
-    depth = lane_pos((8, LANES)) % 16
-    here = rows_of(i)
-    s = [S[k, here, :] for k in range(6)]
-    p = S[6, here, :]
-    light = L[0, here, :]
-    V_to[0, here, :] = V[0, here, :] + light * (
-        along_x(S, 0, i, LANES) + across(s[3], 1, 16) + along_z(s[4], depth, 0.0)
+def z_weights(W):
+    k = lax.broadcasted_iota(jnp.int32, (128, 128), 0)
+    at = lax.broadcasted_iota(jnp.int32, (128, 128), 1)
+    depth = at % 16
+    up = jnp.logical_and(k == at + 1, depth != 15).astype(F32)
+    down = jnp.logical_and(k == at - 1, depth != 0).astype(F32)
+    change = (up - down).astype(BF16)
+    top = jnp.logical_and(k == at - 15, depth == 15).astype(F32)
+    base = jnp.logical_and(k == at + 15, depth == 0).astype(F32)
+    for half, sign in ((0, 1.0), (1, -1.0)):
+        into_brick, into_water = (-sign * top).astype(BF16), (sign * base).astype(BF16)
+        for part in range(2):
+            rows = slice(128 * part, 128 * part + 128)
+            W[half, rows, 0:128], W[half, rows, 128:256] = change, into_water
+            rows = slice(256 + 128 * part, 384 + 128 * part)
+            W[half, rows, 0:128], W[half, rows, 128:256] = into_brick, change
+
+
+def parts(values):
+    out = []
+    for value in values:
+        high = value.astype(BF16)
+        out += [high, (value - high.astype(F32)).astype(BF16)]
+    return jnp.concatenate(out, axis=1)
+
+
+def stacked(ref, f, tiles):
+    return jnp.concatenate(
+        [ref[f, rows_of(i), 128 * t:128 * t + 128] for i, t in tiles], axis=0
     )
-    V_to[1, here, :] = V[1, here, :] + light * (
-        along_x(S, 3, i, LANES) + across(s[1], 1, 16) + along_z(s[5], depth, 0.0)
-    )
-    V_to[2, here, :] = V[2, here, :] + light * (
-        along_x(S, 4, i, LANES) + across(s[5], 1, 16)
-        + along_z(s[2], depth, -shift(p, 15, 1))
-    )
-    light = L[1, here, :]
-    G_to[0, here, :] = G[0, here, :] - light * along_x(S, 6, i, LANES)
-    G_to[1, here, :] = G[1, here, :] - light * across(p, 1, 16)
-    G_to[2, here, :] = G[2, here, :] - light * (
-        shift(p, -1, 1) - jnp.where(depth == 0, -shift(s[2], -15, 1), shift(p, 1, 1))
-    )
-
-
-def brick_stress(i, V, S, G, CF, M, S_to, M_to):
-    depth = lane_pos((8, INNER)) % 16
-    here = rows_of(i)
-    v = [V[k, here, 0:INNER] for k in range(3)]
-    w = G[2, here, 0:INNER]
-    change = along_x(G, 0, i, INNER) + across(G[1, here, :], 1, 16)[:, 0:INNER]
-    change = change + shift(w, -1, 1)
-    change = change - jnp.where(depth == 0, shift(v[2], -15, 1), shift(w, 1, 1))
-    S_to[6, here, 0:INNER] = S[6, here, 0:INNER] - CF[7, here, :] * change
-    dx = [along_x(V, k, i, INNER) for k in range(3)]
-    dy = [across(V[k, here, :], 1, 16)[:, 0:INNER] for k in range(3)]
-    dz = [along_z(v[k], depth, shift(G[k, here, 0:INNER], 15, 1)) for k in range(3)]
-    strain = (
-        dx[0], dy[1], dz[2],
-        0.5 * (dy[0] + dx[1]), 0.5 * (dz[0] + dx[2]), 0.5 * (dz[1] + dy[2]),
-    )
-    dilation = dx[0] + dy[1] + dz[2]
-    for k in range(6):
-        gain = CF[1, here, :] * strain[k]
-        relaxed = CF[6, here, :] * strain[k]
-        if k < 3:
-            gain = gain + CF[0, here, :] * dilation
-            relaxed = relaxed + CF[5, here, :] * dilation
-        for mechanism in range(3):
-            held = M[6 * mechanism + k, here, :]
-            held = relaxed + CF[2 + mechanism, here, :] * (held - relaxed)
-            M_to[6 * mechanism + k, here, :] = held
-            gain = gain - held
-        S_to[k, here, 0:INNER] = S[k, here, 0:INNER] + gain
+
+
+def unstacked(value, tiles, i, count):
+    none = jnp.zeros((8, 128), F32)
+    found = []
+    for t in range(count):
+        if (i, t) in tiles:
+            place = 8 * tiles.index((i, t))
+            found.append(value[place:place + 8])
+        else:
+            found.append(none)
+    return jnp.concatenate(found, axis=1)
+
+
+def times(values, weights):
+    return jnp.dot(parts(values), weights, preferred_element_type=F32)
+
+
+def brick_velocity(group, V, S, G, L, W, V_to, G_to):
+    tiles = [(i, t) for i in group for t in range(5) if (i, t) != (4, 4)]
+    single = W[0, 0:256, 0:128]
+    xz = times([stacked(S, 4, tiles)], single)
+    yz = times([stacked(S, 5, tiles)], single)
+    both = times([stacked(S, 2, tiles), stacked(S, 6, tiles)], W[0])
+    for i in group:
+        here = rows_of(i)
+        light = L[0, here, :]
+        V_to[0, here, :] = V[0, here, :] + light * (
+            along_x(S, 0, i, LANES) + across(S[3, here, :], 1, 16)
+            + unstacked(xz, tiles, i, 5)
+        )
+        V_to[1, here, :] = V[1, here, :] + light * (
+            along_x(S, 3, i, LANES) + across(S[1, here, :], 1, 16)
+            + unstacked(yz, tiles, i, 5)
+        )
+        V_to[2, here, :] = V[2, here, :] + light * (
+            along_x(S, 4, i, LANES) + across(S[5, here, :], 1, 16)
+            + unstacked(both[:, 0:128], tiles, i, 5)
+        )
+        light = L[1, here, :]
+        G_to[0, here, :] = G[0, here, :] - light * along_x(S, 6, i, LANES)
+        G_to[1, here, :] = G[1, here, :] - light * across(S[6, here, :], 1, 16)
+        G_to[2, here, :] = G[2, here, :] - light * unstacked(both[:, 128:256], tiles, i, 5)
+
+
+def brick_stress(group, V, S, G, CF, M, W, S_to, M_to):
+    tiles = [(i, t) for i in group for t in range(4)]
+    pair = W[1, :, 0:128]
+    z_all = [
+        times([stacked(V, 0, tiles), stacked(G, 0, tiles)], pair),
+        times([stacked(V, 1, tiles), stacked(G, 1, tiles)], pair),
+    ]
+    both = times([stacked(V, 2, tiles), stacked(G, 2, tiles)], W[1])
+    z_all.append(both[:, 0:128])
+    for i in group:
+        here = rows_of(i)
+        change = along_x(G, 0, i, INNER) + across(G[1, here, :], 1, 16)[:, 0:INNER]
+        change = change + unstacked(both[:, 128:256], tiles, i, 4)
+        S_to[6, here, 0:INNER] = S[6, here, 0:INNER] - CF[7, here, :] * change
+        dx = [along_x(V, k, i, INNER) for k in range(3)]
+        dy = [across(V[k, here, :], 1, 16)[:, 0:INNER] for k in range(3)]
+        dz = [unstacked(z_all[k], tiles, i, 4) for k in range(3)]
+        strain = (
+            dx[0], dy[1], dz[2],
+            0.5 * (dy[0] + dx[1]), 0.5 * (dz[0] + dx[2]), 0.5 * (dz[1] + dy[2]),
+        )
+        dilation = dx[0] + dy[1] + dz[2]
+        for k in range(6):
+            gain = CF[1, here, :] * strain[k]
+            relaxed = CF[6, here, :] * strain[k]
+            if k < 3:
+                gain = gain + CF[0, here, :] * dilation
+                relaxed = relaxed + CF[5, here, :] * dilation
+            for mechanism in range(3):
+                held = M[6 * mechanism + k, here, :]
+                held = relaxed + CF[2 + mechanism, here, :] * (held - relaxed)
+                M_to[6 * mechanism + k, here, :] = held
+                gain = gain - held
+            S_to[k, here, 0:INNER] = S[k, here, 0:INNER] + gain
 
 
 def main_kernel(
     mvs_in, mem_in, mat_in, live_in, water_in, wmat_in, table,
     V, S, G, L, CF, M, PR, U,
-    C, MAT, WS, WM,
+    C, ZW, MAT, WS, WM,
     tbx, tby, tbc, twx, twy, sbx, sby, swx, swy,
     rbx, rby, rbc, rwx, rwy, ebx, eby, ewx, ewy,
     load_sem, send_sem, recv_sem, xsend_sem, xrecv_sem,
@@ -168,7 +219,7 @@
     kind_load = pltpu.make_async_copy(
         wmat_in, WM.at[:, pl.ds(0, SIDE)], load_sem.at[18]
     )
-    for load in motion_loads + [pressure_load, velocity_load, kind_load] + memory_loads:
+    for load in [pressure_load, velocity_load, kind_load] + motion_loads + memory_loads:
         load.start()
 
     barrier = pltpu.get_barrier_semaphore()
@@ -259,10 +310,11 @@
     def brick_y_copies(n):
         return side_copies(None, (tby.at[n], rby.at[n]), None, step_sems(n, 2))
 
-    def water_copies(n):
-        return side_copies(
-            (twx.at[n], rwx.at[n]), (twy.at[n], rwy.at[n]), step_sems(n, 8), step_sems(n, 10)
-        )
+    def water_x_copies(n):
+        return side_copies((twx.at[n], rwx.at[n]), None, step_sems(n, 8), None)
+
+    def water_y_copies(n):
+        return side_copies(None, (twy.at[n], rwy.at[n]), None, step_sems(n, 10))
 
     def first_water_copies():
         return side_copies((swx, ewx), (swy, ewy), extra_sems(0), extra_sems(2))
@@ -377,10 +429,13 @@
                 tile_lane < 64, shift(eby[1], -16 * j, 1), shift(eby[0], 112 - 16 * j, 1)
             )
 
-    def pack_water(n):
+    def pack_water_x(n):
         for k in range(2):
             twx[n, 0, k] = PR[32 + k, inner, :]
             twx[n, 1, k] = PR[2 + k, inner, :]
+
+    def pack_water_y(n):
+        for k in range(2):
             twy[n, 0, k] = flat_p[line(0, 30 + k), :]
             twy[n, 1, k] = flat_p[line(0, k), :]
 
@@ -392,10 +447,12 @@
             flat_p[line(0, 32 + k), :] = rwy[n, 1, k]
 
     def pack_first_water():
-        swx[0, 0], swx[0, 1] = U[0, 33, inner, :], C[0, 33, inner, :]
-        swx[1, 0], swx[1, 1] = U[0, 2, inner, :], C[0, 2, inner, :]
-        swy[0, 0], swy[0, 1] = flat_u[line(1, 31), :], flat_c[line(0, 31), :]
-        swy[1, 0], swy[1, 1] = flat_u[line(1, 0), :], flat_c[line(0, 0), :]
+        for t in range(2):
+            end = SIDE - 1 if t == 0 else 0
+            swx[t, 0] = U[0, 2 + end, inner, :]
+            swx[t, 1] = 0.5 * pick(WM[end, 0:SIDE, :], table, 0)
+            swy[t, 0] = flat_u[line(1, end), :]
+            swy[t, 1] = 0.5 * pick(flat_m[pl.ds(end, SIDE, stride=PADDED), :], table, 0)
 
     def unpack_first_water():
         U[0, 1, inner, :], C[0, 1, inner, :] = ewx[0, 0], ewx[0, 1]
@@ -417,38 +474,53 @@
     plane_lane = lane_pos((SIDE, 128))
     wide, above_rows, below_rows = pl.ds(7, 40), pl.ds(8, 40), pl.ds(6, 40)
 
-    def water_step():
+    def x_velocity(x_at):
+        U[0, x_at, inner] -= C[0, x_at, inner] * (PR[x_at + 1, inner] - PR[x_at - 1, inner])
+
+    def water_velocity(x_at):
+        x_velocity(x_at)
+        U[1, x_at, wide] -= C[0, x_at, wide] * (PR[x_at, above_rows] - PR[x_at, below_rows])
+        p = PR[x_at, inner]
+        U[2, x_at, inner] -= C[2, x_at, inner] * (
+            jnp.where(plane_lane == 0, 0.0, p) - shift(p, 2, 1)
+        )
+
+    def water_pressure(x_at):
+        change = U[0, x_at + 1, inner] - U[0, x_at - 1, inner]
+        change = change + (U[1, x_at, pl.ds(9, SIDE)] - U[1, x_at, pl.ds(7, SIDE)])
+        w = U[2, x_at, inner]
+        change = change + (jnp.where(plane_lane == 127, 0.0, shift(w, -2, 1)) - w)
+        PR[x_at, inner] -= C[1, x_at, inner] * change
+
+    def water_ends():
+        x_velocity(1)
+        x_velocity(34)
+        for x_at in (2, 3, 4, 5, 30, 31, 32, 33):
+            water_velocity(x_at)
+        for x_at in (2, 3, 32, 33):
+            water_pressure(x_at)
+
+    def water_rest():
         def velocity(x, carry):
             for plane in range(4):
-                x_at = 4 * x + (2 + plane)
-                p, light = PR[x_at, inner], C[0, x_at, inner]
-                U[0, x_at, inner] -= light * (PR[x_at + 1, inner] - PR[x_at - 1, inner])
-                U[1, x_at, wide] -= C[0, x_at, wide] * (
-                    PR[x_at, above_rows] - PR[x_at, below_rows]
-                )
-                U[2, x_at, inner] -= C[2, x_at, inner] * (
-                    jnp.where(plane_lane == 0, 0.0, p) - shift(p, 2, 1)
-                )
+                water_velocity(4 * x + (6 + plane))
             return carry
 
-        lax.fori_loop(0, SIDE // 4, velocity, 0)
-        for x_at in (1, 34):
-            U[0, x_at, inner] -= C[0, x_at, inner] * (
-                PR[x_at + 1, inner] - PR[x_at - 1, inner]
-            )
+        lax.fori_loop(0, 6, velocity, 0)
 
         def pressure(x, carry):
             for plane in range(4):
-                x_at = 4 * x + (2 + plane)
-                change = U[0, x_at + 1, inner] - U[0, x_at - 1, inner]
-                change = change + (U[1, x_at, pl.ds(9, SIDE)] - U[1, x_at, pl.ds(7, SIDE)])
-                w = U[2, x_at, inner]
-                change = change + (jnp.where(plane_lane == 127, 0.0, shift(w, -2, 1)) - w)
-                PR[x_at, inner] -= C[1, x_at, inner] * change
+                water_pressure(4 * x + (4 + plane))
             return carry
 
-        lax.fori_loop(0, SIDE // 4, pressure, 0)
-
+        lax.fori_loop(0, 7, pressure, 0)
+
+    pressure_load.wait()
+    velocity_load.wait()
+    kind_load.wait()
+    pack_water_x(0)
+    pack_water_y(0)
+    pack_first_water()
     for load in motion_loads:
         load.wait()
     live = [live_in[s].astype(F32) for s in range(4)]
@@ -473,7 +545,6 @@
         return carry
 
     lax.fori_loop(0, 4, motion_start, 0)
-    pressure_load.wait()
     to_slab(S, 6, lambda y: flat_p[line(0, y), :])
     pack_brick_x(0)
     pack_brick_y(0)
@@ -481,10 +552,11 @@
     for there in partners[1:]:
         count = count + there.astype(jnp.int32)
     pl.semaphore_wait(barrier, count)
+    start(water_x_copies(0))
+    start(water_y_copies(0))
+    start(first_water_copies())
     start(brick_x_copies(0))
     start(brick_y_copies(0))
-    velocity_load.wait()
-    kind_load.wait()
     to_slab(G, 0, lambda y: flat_u[line(0, y), :])
     to_slab(G, 1, lambda y: flat_u[line(1, y), :])
     to_slab(WS, None, lambda y: flat_m[pl.ds(y, SIDE, stride=PADDED), :])
@@ -498,9 +570,8 @@
     lax.fori_loop(0, 4, slab_params, 0)
     pack_first_brick()
     start(first_brick_copies())
-    pack_water(0)
-    start(water_copies(0))
     to_slab(G, 2, lambda y: flat_u[line(2, y), :])
+    z_weights(ZW)
 
     def water_params(x, carry):
         for plane in range(2):
@@ -514,8 +585,6 @@
         return carry
 
     lax.fori_loop(0, SIDE // 2, water_params, 0)
-    pack_first_water()
-    start(first_water_copies())
     for load in memory_loads:
         load.wait()
 
@@ -538,11 +607,15 @@
     unpack_first_water()
 
     def step(n, carry):
-        arrive(water_copies(n))
+        arrive(water_y_copies(n))
+        arrive(water_x_copies(n))
         unpack_water(n)
-        water_step()
-        pack_water(n + 1)
-        start(water_copies(n + 1))
+        water_ends()
+        pack_water_x(n + 1)
+        start(water_x_copies(n + 1))
+        water_rest()
+        pack_water_y(n + 1)
+        start(water_y_copies(n + 1))
 
         @pl.when(n == 0)
         def _():
@@ -551,27 +624,25 @@
 
         arrive(brick_y_copies(n))
         unpack_brick_y(n)
-        for i in (1, 2):
-            brick_velocity(i, V, S, G, L, V, G)
+        brick_velocity((1, 2), V, S, G, L, ZW, V, G)
         arrive(brick_x_copies(n))
         unpack_brick_x(n)
-        for i in (0, 3, 4):
-            brick_velocity(i, V, S, G, L, V, G)
-        for i in (0, 3):
-            brick_stress(i, V, S, G, CF, M, S, M)
+        brick_velocity((0, 3, 4), V, S, G, L, ZW, V, G)
+        brick_stress((0, 3), V, S, G, CF, M, ZW, S, M)
         pack_brick_x(n + 1)
         start(brick_x_copies(n + 1))
-        for i in (1, 2):
-            brick_stress(i, V, S, G, CF, M, S, M)
+        brick_stress((1, 2), V, S, G, CF, M, ZW, S, M)
         pack_brick_y(n + 1)
         start(brick_y_copies(n + 1))
         return carry
 
     lax.fori_loop(0, STEPS - 1, step, 0)
     last = STEPS - 1
-    arrive(water_copies(last))
+    arrive(water_y_copies(last))
+    arrive(water_x_copies(last))
     unpack_water(last)
-    water_step()
+    water_ends()
+    water_rest()
 
     def settle(x, carry):
         for plane in range(4):
@@ -583,7 +654,8 @@
     sent(first_water_copies())
     sent(first_brick_copies())
     for n in range(STEPS):
-        sent(water_copies(n))
+        sent(water_x_copies(n))
+        sent(water_y_copies(n))
         sent(brick_x_copies(n))
         sent(brick_y_copies(n))
     arrive(brick_y_copies(last))
@@ -595,12 +667,11 @@
 def last_kernel(
     V, S, G, L, CF, M, PR, U,
     motion_out, memory_out, water_out,
-    V_to, G_to, S_to, M_to, W_to, sem,
+    V_to, G_to, S_to, M_to, W_to, ZW, sem,
 ):
-    for i in range(5):
-        brick_velocity(i, V, S, G, L, V_to, G_to)
-    for i in range(4):
-        brick_stress(i, V_to, S, G_to, CF, M, S_to, M_to)
+    z_weights(ZW)
+    brick_velocity((0, 1, 2, 3, 4), V, S, G, L, ZW, V_to, G_to)
+    brick_stress((0, 1, 2, 3), V_to, S, G_to, CF, M, ZW, S_to, M_to)
     stores = []
     for s in range(4):
         rows, lanes = pl.ds(EDGE * (s // 2), EDGE), pl.ds(256 * (s % 2), 256)
@@ -664,6 +735,7 @@
         out_specs=(vmem,) * len(state),
         scratch_shapes=[
             pltpu.VMEM((3, PLANES, DEEP, 128), F32),
+            pltpu.VMEM((2, 512, 256), BF16),
             pltpu.VMEM((SIDE, INNER), jnp.int32),
             pltpu.VMEM((SIDE, INNER), jnp.int32),
             pltpu.VMEM((SIDE, PADDED, 128), jnp.int32),
@@ -695,6 +767,7 @@
             pltpu.VMEM((7, SIDE, INNER), F32),
             pltpu.VMEM((18, SIDE, INNER), F32),
             pltpu.VMEM((4, SIDE, PADDED, 128), F32),
+            pltpu.VMEM((2, 512, 256), BF16),
             pltpu.SemaphoreType.DMA((16,)),
         ],
         compiler_params=pltpu.CompilerParams(vmem_limit_bytes=24 << 20),

time: 34.5 us -> 31.6 us (0.916)
  Pallas kernels: 33.7 us -> 30.5 us
    pallas_call x1, Pallas kernels: 30.7 us -> 27.7 us  [body(): pl.pallas_call(main_kernel, out_shape=tuple((pltpu.VMEM(shape, F32) for s...]
where the time goes in v2:
time: 31.6 us; the launch traced here: 31.2 us
  Pallas kernels  30.5 us (97%)
  between operations  0.64 us (2%)
    pallas_call x1, Pallas kernels, body(): pl.pallas_call(main_kernel, out_shape=tuple((pltpu.VMEM(shape, F32) for s...  27.7 us
    pallas_call x1, Pallas kernels, body(): pl.pallas_call(last_kernel, out_shape=(jax.ShapeDtypeStruct((4, 9, EDGE,...  2.87 us

profile of v2, /device:TPU:24, one launch (start us, length us, event | category | flops | bytes accessed | tf_op | source)
XLA Modules:
  0.0 31.2 jit_solution(3092708495794128352)
XLA Ops:
  0.6 27.7 %ultrasound_steps.1 = (f32[3,40,640]{2,1,0:T(8,128)S(1)}, f32[7,40,640]{2,1,0:T(8,128)S(1)}, f32[3,40,640]{2,1,0:T(8,128)S(1)}, f32[2,40,640]{2,1,0:T(8,128)S(1)...) custom-call(f32[4,9,16,256]{3,2,1,0:T(8,128)} %mvs_in.1, ...), custom_call_target="tpu_custom_call" | custom-call | tf_op jit(solution)/shard_map/ultrasound_steps/pallas_call | solution.py:731
  28.3 2.9 %ultrasound_last.1 = (f32[4,9,16,256]{3,2,1,0:T(8,128)}, f32[4,18,16,256]{3,2,1,0:T(8,128)}, f32[4,32,32,128]{3,2,1,0:T(8,128)}) custom-call(f32[3,40,640]{2,1,0:T(8,128)S(1)} %get-tuple-element.11.V, f32[7,40,640]{2,1,0:T(8,128)S(1)} %get-tuple-element.12.S, f32[3,40,640]{2,1,0:T(8,128)S(1)} %get-tuple-element.13.G, f32[2,40,640]{2,1,0:T(8,128)S(1)} %get-tuple-element.14.L, ...), custom_call_target="tpu_custom_call" | custom-call | tf_op jit(solution)/shard_map/ultrasound_last/pallas_call | solution.py:755

commit v3 on v2

--- a/solution.py
+++ b/solution.py
@@ -670,22 +670,33 @@
     V_to, G_to, S_to, M_to, W_to, ZW, sem,
 ):
     z_weights(ZW)
-    brick_velocity((0, 1, 2, 3, 4), V, S, G, L, ZW, V_to, G_to)
-    brick_stress((0, 1, 2, 3), V_to, S, G_to, CF, M, ZW, S_to, M_to)
+    for group in ((0, 1), (2, 3), (4,)):
+        brick_velocity(group, V, S, G, L, ZW, V_to, G_to)
     stores = []
-    for s in range(4):
-        rows, lanes = pl.ds(EDGE * (s // 2), EDGE), pl.ds(256 * (s % 2), 256)
-        stores += [
-            pltpu.make_async_copy(
-                V_to.at[:, rows, lanes], motion_out.at[s, pl.ds(0, 3)], sem.at[s]
-            ),
-            pltpu.make_async_copy(
-                S_to.at[pl.ds(0, 6), rows, lanes], motion_out.at[s, pl.ds(3, 6)], sem.at[4 + s]
-            ),
-            pltpu.make_async_copy(M_to.at[:, rows, lanes], memory_out.at[s], sem.at[8 + s]),
-        ]
-    for store in stores:
-        store.start()
+
+    def store(half):
+        for s in (2 * half, 2 * half + 1):
+            rows, lanes = pl.ds(EDGE * half, EDGE), pl.ds(256 * (s % 2), 256)
+            for copy in (
+                pltpu.make_async_copy(
+                    V_to.at[:, rows, lanes], motion_out.at[s, pl.ds(0, 3)], sem.at[s]
+                ),
+                pltpu.make_async_copy(
+                    S_to.at[pl.ds(0, 6), rows, lanes], motion_out.at[s, pl.ds(3, 6)],
+                    sem.at[4 + s],
+                ),
+                pltpu.make_async_copy(
+                    M_to.at[:, rows, lanes], memory_out.at[s], sem.at[8 + s]
+                ),
+            ):
+                copy.start()
+                stores.append(copy)
+
+    for half in range(2):
+        brick_stress(
+            (2 * half, 2 * half + 1), V_to, S, G_to, CF, M, ZW, S_to, M_to
+        )
+        store(half)
     tile_lane = lane_pos((SIDE, 128))
     flat_p = PR.reshape(PLANES * DEEP, 128)
     flat_u = U.reshape(3 * PLANES * DEEP, 128)
@@ -709,8 +720,8 @@
             )
         )
         stores[-1].start()
-    for store in stores:
-        store.wait()
+    for copy in stores:
+        copy.wait()
 
 
 def body(*args):

time: 31.6 us -> 31.5 us (level)
  no operation moved by 1% of the time
where the time goes in v3:
time: 31.5 us; the launch traced here: 31.1 us
  Pallas kernels  30.5 us (97%)
  between operations  0.64 us (2%)
    pallas_call x1, Pallas kernels, body(): pl.pallas_call(main_kernel, out_shape=tuple((pltpu.VMEM(shape, F32) for s...  27.7 us
    pallas_call x1, Pallas kernels, body(): pl.pallas_call(last_kernel, out_shape=(jax.ShapeDtypeStruct((4, 9, EDGE,...  2.82 us

profile of v3, /device:TPU:24, one launch (start us, length us, event | category | flops | bytes accessed | tf_op | source)
XLA Modules:
  0.0 31.1 jit_solution(3736767822081905512)
XLA Ops:
  0.6 27.7 %ultrasound_steps.1 = (f32[3,40,640]{2,1,0:T(8,128)S(1)}, f32[7,40,640]{2,1,0:T(8,128)S(1)}, f32[3,40,640]{2,1,0:T(8,128)S(1)}, f32[2,40,640]{2,1,0:T(8,128)S(1)...) custom-call(f32[4,9,16,256]{3,2,1,0:T(8,128)} %mvs_in.1, ...), custom_call_target="tpu_custom_call" | custom-call | tf_op jit(solution)/shard_map/ultrasound_steps/pallas_call | solution.py:742
  28.3 2.8 %ultrasound_last.1 = (f32[4,9,16,256]{3,2,1,0:T(8,128)}, f32[4,18,16,256]{3,2,1,0:T(8,128)}, f32[4,32,32,128]{3,2,1,0:T(8,128)}) custom-call(f32[3,40,640]{2,1,0:T(8,128)S(1)} %get-tuple-element.11.V, f32[7,40,640]{2,1,0:T(8,128)S(1)} %get-tuple-element.12.S, f32[3,40,640]{2,1,0:T(8,128)S(1)} %get-tuple-element.13.G, f32[2,40,640]{2,1,0:T(8,128)S(1)} %get-tuple-element.14.L, ...), custom_call_target="tpu_custom_call" | custom-call | tf_op jit(solution)/shard_map/ultrasound_last/pallas_call | solution.py:766
